TPU v7x, 256 devices: a whole 4x4x8 slice. The times are simulated.
256 devices in a mesh: sub: 8 (over z), row: 2 (over core), col: 16 (over y, x).
Axes of the slice: x: 4, y: 4, z: 8, core: 2. Of those that a mesh axis runs over, the one named last changes fastest.
Arguments:
- factor_cols: bfloat16 [8, 2, 2048, 4096], P('sub', None, 'col', 'row'), may hold values from -0.09375 to 0.09375
- block_pattern: int32 [8, 16, 16], P('sub'), may hold values 0 or 1
- diag_inverse: float32 [8, 4096, 2048], P('sub', ('row', 'col')), may hold values from -1 to 2
- coupling_cols: bfloat16 [8, 2, 2048, 1024], P('sub', 'row', 'col'), may hold values from -0.09375 to 0.09375
- separator_rows: int32 [8, 1024], P('sub'), may hold values from 0 to 1535, as said below
- root_inverse: float32 [1536, 1536], P('col'), may hold values from -1 to 2
- right_side: float32 [8, 4096, 128], P('sub', 'row'), may hold values from -6 to 6
- root_right: float32 [1536, 128], P('col'), may hold values from -6 to 6
Outputs:
- solution: float32 [8, 4096, 128], P('sub', ('row', 'col'))
- root_solution: float32 [1536, 128], P('col')
Inputs may be any that keep to these rules, and one draw needn't show every extreme that they name: `separator_rows`: within one section the 1024 entries are distinct.
All inputs are finite; a program needn't handle non-finite values. No bound on the sum of `block_pattern` on one device may be relied on, other than what follows from the above.
Results may differ from a plain program's by a relative error of at most 0.003.
Values may be sent and summed in bfloat16 or wider, within the bound.
No kernel may reach another device: no remote copies, remote signals or barrier semaphores. Data moves between devices by JAX's collectives and lax.ppermute only.
A program may use at most 64 MiB of HBM per device.

v0:
```python
import jax
import jax.numpy as jnp
from jax import lax
from jax.sharding import PartitionSpec as P

BLOCK = 256
SEPARATOR = 1536
precise = lax.Precision.HIGHEST
first_axes = (((0,), (0,)), ((), ()))


def spread(block, axis, source):
    block = jnp.where(lax.axis_index(axis) == source, block, jnp.zeros_like(block))
    return lax.psum(block, axis)


def shards(
    factor_cols,
    block_pattern,
    diag_inverse,
    coupling_cols,
    separator_rows,
    root_inverse,
    right_side,
    root_right,
):
    factor = factor_cols[0]
    table = block_pattern[0]
    inverse = diag_inverse[0]
    couple_own = coupling_cols[0, 0]
    right_rows = right_side[0]
    rows_sep = separator_rows[0]
    panel_count, col_width, panel_rows = factor.shape
    sources = right_rows.shape[1]
    block_count = table.shape[1]
    row_id = lax.axis_index("row")
    col_id = lax.axis_index("col")
    sub_id = lax.axis_index("sub")
    own_blocks = lax.dynamic_slice_in_dim(
        table, row_id * (panel_rows // BLOCK), panel_rows // BLOCK, 0
    ).astype(jnp.float32)
    row_mask = jnp.repeat(own_blocks, BLOCK, axis=0)
    col_pos = (
        jnp.arange(panel_count)[:, None] * panel_rows
        + col_id * col_width
        + jnp.arange(col_width)[None, :]
    )
    selector = (jnp.arange(block_count)[:, None, None] == (col_pos // BLOCK)[None]).astype(
        jnp.float32
    )
    pattern_mask = jnp.einsum("in,nqj->qji", row_mask, selector)
    below_mask = (jnp.arange(panel_count) < row_id).astype(jnp.float32)[:, None, None]
    masked = factor * (pattern_mask * below_mask).astype(jnp.bfloat16)
    zero_panel = jnp.zeros((panel_rows, sources), jnp.float32)
    zero_share = jnp.zeros((col_width, sources), jnp.float32)

    def forward(current, carried):
        accumulated, solved = carried
        panel_total = lax.psum(accumulated, "col")
        solved = lax.cond(
            row_id == current,
            lambda values: jnp.dot(
                inverse, right_rows - values, precision=precise, preferred_element_type=jnp.float32
            ),
            lambda values: solved,
            panel_total,
        )
        received = spread(solved.astype(jnp.bfloat16), "row", current)
        factor_now = lax.dynamic_index_in_dim(masked, current, 0, keepdims=False)
        accumulated = accumulated + lax.dot_general(
            factor_now, received, first_axes, preferred_element_type=jnp.float32
        )
        return (accumulated, solved)

    accumulated, solved = lax.fori_loop(0, panel_count, forward, (zero_panel, zero_share))
    own_low = solved.astype(jnp.bfloat16)
    sep_partial = lax.dot_general(
        couple_own, own_low, first_axes, preferred_element_type=jnp.float32
    )
    onehot = (jnp.arange(SEPARATOR)[:, None] == rows_sep[None, :]).astype(jnp.float32)
    mapped = jnp.dot(onehot, sep_partial, precision=precise, preferred_element_type=jnp.float32)
    share_rows = root_inverse.shape[0]
    slice_start = col_id * share_rows
    first_device = ((sub_id == 0) & (row_id == 0)).astype(jnp.float32)
    own_rows = (
        lax.dynamic_slice_in_dim(-mapped, slice_start, share_rows, 0) + first_device * root_right
    )
    root_term = lax.dynamic_update_slice_in_dim(-mapped, own_rows, slice_start, 0)
    root_rhs = lax.psum(root_term, ("sub", "row", "col"))
    root_half = jnp.dot(
        root_inverse, root_rhs, precision=precise, preferred_element_type=jnp.float32
    )
    root_part = lax.psum_scatter(
        lax.dot_general(
            root_inverse,
            root_half,
            first_axes,
            precision=precise,
            preferred_element_type=jnp.float32,
        ),
        "col",
        scatter_dimension=0,
        tiled=True,
    )
    root_full = lax.all_gather(root_part.astype(jnp.bfloat16), "col", axis=0, tiled=True).astype(
        root_part.dtype
    )
    picked = lax.dot_general(
        onehot, root_full, first_axes, precision=precise, preferred_element_type=jnp.float32
    ).astype(jnp.bfloat16)
    couple_back = jnp.dot(couple_own, picked, preferred_element_type=jnp.float32)

    def backward(counter, carried):
        finished, panel_low = carried
        current = panel_count - 1 - counter
        factor_now = lax.dynamic_index_in_dim(masked, current, 0, keepdims=False)
        contribution = jnp.dot(factor_now, panel_low, preferred_element_type=jnp.float32)
        own_couple = couple_back * (row_id == current).astype(jnp.float32)
        summed = lax.psum(contribution + own_couple, "row")
        partial_value = lax.cond(
            row_id == current,
            lambda values: lax.dot_general(
                inverse,
                solved - values,
                first_axes,
                precision=precise,
                preferred_element_type=jnp.float32,
            ),
            lambda values: zero_panel,
            summed,
        )
        value = lax.psum_scatter(partial_value, "col", scatter_dimension=0, tiled=True)
        whole_low = lax.all_gather(value.astype(jnp.bfloat16), "col", axis=0, tiled=True)
        active = row_id == current
        finished = jnp.where(active, value, finished)
        panel_low = jnp.where(active, whole_low, panel_low)
        return (finished, panel_low)

    finished, panel_low = lax.fori_loop(
        0, panel_count, backward, (zero_share, zero_panel.astype(jnp.bfloat16))
    )
    return (finished[None], root_part)


def solution(mesh):
    return jax.shard_map(
        shards,
        mesh=mesh,
        in_specs=(
            P("sub", None, "col", "row"),
            P("sub", None, None),
            P("sub", ("row", "col"), None),
            P("sub", "row", "col", None),
            P("sub", None),
            P("col", None),
            P("sub", "row", None),
            P("col", None),
        ),
        out_specs=(P("sub", ("row", "col"), None), P("col", None)),
        check_vma=False,
    )
```

profile of v0, /device:TPU:32, one launch (start us, length us, event | category | flops | bytes accessed | tf_op | source)
XLA Modules:
  0.0 886.8 jit_solution(2642969435639359948)
XLA Ops:
  9.1 2.8 fusion.15
  11.9 221.9 %while.37 = (s32[]{:T(128)}, f32[2048,128]{1,0:T(8,128)}, f32[128,128]{0,1:T(8,128)S(1)}, bf16[2,128,2048]{2,1,0:T(8,128)(2,1)}, s32[]{:T(128)}, /*index=5*/f32[...) while((s32[]{:T(128)}, f32[2048,128]{1,0:T(8,128)}, ...), condition=%wide.region_5.6_spmd.clone, body=%wide.region_0.5_spmd.clone.sunk | while | flops 470859776 | bytes 18612512 | solution.py:75
  12.0 1.1 broadcast_select_fusion.7
  13.1 103.1 %all-reduce.6.cloned.1.call-done = f32[2048,128]{1,0:T(8,128)} async-done(((f32[2048,128]{1,0:T(8,128)}), f32[2048,128]{1,0:T(8,128)}) %all-reduce.6.cloned.1.call-update) | async-done | bytes 1048592 | tf_op jit(solution)/shard_map/while/body/eval_jaxpr/psum | solution.py:59
  116.2 3.5 conditional.7
  116.2 3.5 convolution_bitcast_fusion.1
  119.7 3.4 psum.51
  123.1 2.4 convolution_add_fusion.4
  125.5 2.3 broadcast_select_fusion.7
  127.8 98.6 %all-reduce.6.cloned.1.call-done = f32[2048,128]{1,0:T(8,128)} async-done(((f32[2048,128]{1,0:T(8,128)}), f32[2048,128]{1,0:T(8,128)}) %all-reduce.6.cloned.1.call-update) | async-done | bytes 1048592 | tf_op jit(solution)/shard_map/while/body/eval_jaxpr/psum | solution.py:59
  226.4 5.1 psum.51
  231.4 2.4 convolution_add_fusion.4
  234.0 2.9 fusion.16
  238.0 252.3 %all-reduce.4.cloned.1.call-done = f32[1536,128]{1,0:T(8,128)} async-done(((f32[1536,128]{1,0:T(8,128)}), f32[1536,128]{1,0:T(8,128)}) %all-reduce.4.cloned.1.call-update) | async-done | bytes 786448 | tf_op jit(solution)/shard_map/psum | solution.py:89
  490.3 1.9 fusion.24
  493.0 1.2 copy.27
  494.3 79.0 %reduce-scatter.5.cloned.1.call-done = f32[96,128]{1,0:T(8,128)} async-done(((f32[1536,128]{1,0:T(8,128)}), f32[96,128]{1,0:T(8,128)}) %reduce-scatter.5.cloned.1.call-update) | async-done | bytes 49168 | tf_op jit(solution)/shard_map/reduce_scatter | solution.py:93
  574.2 23.4 %all_gather.13 = bf16[1536,128]{1,0:T(8,128)(2,1)S(1)} all-gather(bf16[96,128]{1,0:T(8,128)(2,1)S(1)} %convert_element_type.87), channel_id=1, replica_groups=mesh['sub'=8,'row'=2,'col'=16] {'col'}, dimensions={0}, use_global_device_ids=true | all-gather | bytes 417792 | tf_op jit(solution)/shard_map/all_gather | solution.py:105
  597.6 1.8 fusion.17
  599.7 278.9 %while.38 = (s32[]{:T(128)}, f32[128,128]{0,1:T(8,128)S(1)}, bf16[2048,128]{0,1:T(8,128)(2,1)S(1)}, s32[]{:T(128)}, bf16[2,128,2048]{2,1,0:T(8,128)(2,1)}, /*ind...) while((s32[]{:T(128)}, f32[128,128]{0,1:T(8,128)S(1)}, ...), condition=%wide.region_13.14_spmd.clone, body=%wide.region_8.13_spmd.clone.sunk | while | flops 470663168 | bytes 13697360 | solution.py:139
  599.8 2.0 convolution_add_fusion.5
  601.9 29.3 %all-reduce.8.cloned.1.call-done = f32[128,128]{1,0:T(8,128)} async-done(((f32[128,128]{1,0:T(8,128)}), f32[128,128]{1,0:T(8,128)}) %all-reduce.8.cloned.1.call-update) | async-done | bytes 65552 | tf_op jit(solution)/shard_map/while/body/eval_jaxpr/psum | solution.py:119
  631.3 1.0 copy-done.3
  632.3 81.8 %reduce-scatter.7.cloned.1.call-done = f32[128,128]{0,1:T(8,128)} async-done(((f32[2048,128]{0,1:T(8,128)}), f32[128,128]{0,1:T(8,128)}) %reduce-scatter.7.cloned.1.call-update) | async-done | bytes 65552 | tf_op jit(solution)/shard_map/while/body/eval_jaxpr/reduce_scatter | solution.py:132
  715.1 24.0 %all_gather.16 = bf16[2048,128]{0,1:T(8,128)(2,1)S(1)} all-gather(bf16[128,128]{0,1:T(8,128)(2,1)S(1)} %get-tuple-element.583), channel_id=1, replica_groups=mesh['sub'=8,'row'=2,'col'=16] {'col'}, dimensions={0}, use_global_device_ids=true | all-gather | bytes 557056 | tf_op jit(solution)/shard_map/while/body/eval_jaxpr/all_gather | solution.py:133
  739.4 2.0 convolution_add_fusion.5
  741.5 29.0 %all-reduce.8.cloned.1.call-done = f32[128,128]{1,0:T(8,128)} async-done(((f32[128,128]{1,0:T(8,128)}), f32[128,128]{1,0:T(8,128)}) %all-reduce.8.cloned.1.call-update) | async-done | bytes 65552 | tf_op jit(solution)/shard_map/while/body/eval_jaxpr/psum | solution.py:119
  770.5 1.9 conditional.8
  770.5 1.9 convolution_bitcast_fusion
  772.4 1.0 copy-done.3
  773.4 80.0 %reduce-scatter.7.cloned.1.call-done = f32[128,128]{0,1:T(8,128)} async-done(((f32[2048,128]{0,1:T(8,128)}), f32[128,128]{0,1:T(8,128)}) %reduce-scatter.7.cloned.1.call-update) | async-done | bytes 65552 | tf_op jit(solution)/shard_map/while/body/eval_jaxpr/reduce_scatter | solution.py:132
  854.4 24.0 %all_gather.16 = bf16[2048,128]{0,1:T(8,128)(2,1)S(1)} all-gather(bf16[128,128]{0,1:T(8,128)(2,1)S(1)} %get-tuple-element.583), channel_id=1, replica_groups=mesh['sub'=8,'row'=2,'col'=16] {'col'}, dimensions={0}, use_global_device_ids=true | all-gather | bytes 557056 | tf_op jit(solution)/shard_map/while/body/eval_jaxpr/all_gather | solution.py:133
  (62 shorter events, 7.9 us)
Async XLA Ops:
  8.0 482.3 %copy-start = (f32[96,1536]{1,0:T(8,128)S(1)}, f32[96,1536]{1,0:T(8,128)}, u32[]{:S(2)}) copy-start(f32[96,1536]{1,0:T(8,128)} %param.21) | copy-start | bytes 1769476
  9.1 2.8 copy-start.2
  11.9 221.9 %copy-start.4 = (bf16[1,1,128,1024]{3,2,1,0:T(8,128)(2,1)S(1)}, bf16[1,1,128,1024]{3,2,1,0:T(8,128)(2,1)}, u32[]{:S(2)}) copy-start(bf16[1,1,128,1024]{3,2,1,0:T(8,128)(2,1)} %param.19) | copy-start | bytes 786436
  11.9 222.1 %copy-start.7 = (s32[1,1024]{1,0:T(1,128)S(1)}, s32[1,1024]{1,0:T(1,128)}, u32[]{:S(2)}) copy-start(s32[1,1024]{1,0:T(1,128)} %param.20) | copy-start | bytes 12292
  11.9 104.2 %all-reduce.6.cloned.1.call-start = ((), (), s32[]{:S(2)}) async-start(), calls=%async_computation.4 | async-start | bytes 2097152 | tf_op jit(solution)/shard_map/while/body/eval_jaxpr/psum | solution.py:59
  116.2 6.9 copy-start.1
  125.5 100.9 %all-reduce.6.cloned.1.call-start = ((), (), s32[]{:S(2)}) async-start(), calls=%async_computation.4 | async-start | bytes 2097152 | tf_op jit(solution)/shard_map/while/body/eval_jaxpr/psum | solution.py:59
  226.4 5.1 copy-start.1
  233.8 256.5 %all-reduce.4.cloned.1.call-start = ((), (), s32[]{:S(2)}) async-start(), calls=%async_computation.2 | async-start | bytes 1572864 | tf_op jit(solution)/shard_map/psum | solution.py:89
  234.0 2.9 copy-start.6
  237.0 0.9 copy-start.5
  237.9 335.5 %reduce-scatter.5.cloned.1.call-start = ((), (), s32[]{:S(2)}) async-start(), calls=%async_computation.3 | async-start | bytes 835584 | tf_op jit(solution)/shard_map/reduce_scatter | solution.py:93
  599.8 31.4 %all-reduce.8.cloned.1.call-start = ((), (), s32[]{:S(2)}) async-start(), calls=%async_computation.5 | async-start | bytes 131072 | tf_op jit(solution)/shard_map/while/body/eval_jaxpr/psum | solution.py:119
  601.8 112.3 %reduce-scatter.7.cloned.1.call-start = ((), (), s32[]{:S(2)}) async-start(), calls=%async_computation.6 | async-start | bytes 1114112 | tf_op jit(solution)/shard_map/while/body/eval_jaxpr/reduce_scatter | solution.py:132
  631.3 1.0 copy-start.3
  739.4 31.1 %all-reduce.8.cloned.1.call-start = ((), (), s32[]{:S(2)}) async-start(), calls=%async_computation.5 | async-start | bytes 131072 | tf_op jit(solution)/shard_map/while/body/eval_jaxpr/psum | solution.py:119
  741.4 112.0 %reduce-scatter.7.cloned.1.call-start = ((), (), s32[]{:S(2)}) async-start(), calls=%async_computation.6 | async-start | bytes 1114112 | tf_op jit(solution)/shard_map/while/body/eval_jaxpr/reduce_scatter | solution.py:132
  772.4 1.0 copy-start.3
Sparse Core Ops, SparseCore 0:
  16.4 99.7 all-reduce.5
  129.9 96.4 all-reduce.5
  603.9 27.2 all-reduce.7
  635.0 79.1 reduce-scatter.6
  743.2 27.2 all-reduce.7
  774.3 79.1 reduce-scatter.6
Sparse Core Ops, SparseCore 1:
  239.7 250.5 all-reduce.3
  494.6 78.7 reduce-scatter.4
where the time goes:
time: 888 us; the launch traced here: 887 us
  waiting for transfers between devices  753 us (85%)
  blocking collectives  79.9 us (9%)
  matrix products  24.7 us (3%)
  between operations  15.7 us (2%)
    psum x1, waiting for transfers between devices, shards(): root_rhs = lax.psum(root_term, ('sub', 'row', 'col'))  252 us
    psum x2, waiting for transfers between devices, forward(): panel_total = lax.psum(accumulated, 'col')  202 us
    reduce_scatter x2, waiting for transfers between devices, backward(): lax.psum_scatter(partial_value, 'col', scatter_dimension=0, tiled=True)  162 us
    reduce_scatter x1, waiting for transfers between devices, shards(): lax.psum_scatter(lax.dot_general(root_inverse, root_half, first_axes, pre...  79 us
    psum x2, waiting for transfers between devices, backward(): summed = lax.psum(contribution + own_couple, 'row')  58.3 us
    all_gather x2, blocking collectives, backward(): lax.all_gather(value.astype(jnp.bfloat16), 'col', axis=0, tiled=True)  48.1 us
    all_gather x1, blocking collectives, shards(): lax.all_gather(root_part.astype(jnp.bfloat16), 'col', axis=0, tiled=True)  23.4 us
  transfers between devices with their start and end apart: 8, of which 8 were waited for; matrix products, arithmetic and copies ran while one was open for 0% of the time, Pallas kernels for 0%

commit v1 on v0

--- a/solution.py
+++ b/solution.py
@@ -56,7 +56,7 @@
 
     def forward(current, carried):
         accumulated, solved = carried
-        panel_total = lax.psum(accumulated, "col")
+        panel_total = jnp.sum(lax.all_gather(accumulated, "col"), axis=0)
         solved = lax.cond(
             row_id == current,
             lambda values: jnp.dot(

time: 888 us -> 940 us (1.059)
  waiting for transfers between devices: 753 us -> 791 us
  other arithmetic: 7.35 us -> 20.6 us
    all_gather x0 -> x2, waiting for transfers between devices: none -> 239 us  [forward(): panel_total = jnp.sum(lax.all_gather(accumulated, 'col'), axis=0)]
    psum x2 -> x0, waiting for transfers between devices: 202 us -> none  [forward(): panel_total = lax.psum(accumulated, 'col')]
    reduce_sum x0 -> x2, other arithmetic: none -> 13.3 us  [forward(): panel_total = jnp.sum(lax.all_gather(accumulated, 'col'), axis=0)]
where the time goes in v1:
time: 940 us; the launch traced here: 939 us
  waiting for transfers between devices  791 us (84%)
  blocking collectives  81.3 us (9%)
  matrix products  24.6 us (3%)
  other arithmetic  20.6 us (2%)
  between operations  15.7 us (2%)
    psum x1, waiting for transfers between devices, shards(): root_rhs = lax.psum(root_term, ('sub', 'row', 'col'))  253 us
    all_gather x2, waiting for transfers between devices, forward(): panel_total = jnp.sum(lax.all_gather(accumulated, 'col'), axis=0)  239 us
    reduce_scatter x2, waiting for transfers between devices, backward(): lax.psum_scatter(partial_value, 'col', scatter_dimension=0, tiled=True)  162 us
    reduce_scatter x1, waiting for transfers between devices, shards(): lax.psum_scatter(lax.dot_general(root_inverse, root_half, first_axes, pre...  79.1 us
    psum x2, waiting for transfers between devices, backward(): summed = lax.psum(contribution + own_couple, 'row')  58.3 us
    all_gather x2, blocking collectives, backward(): lax.all_gather(value.astype(jnp.bfloat16), 'col', axis=0, tiled=True)  48.1 us
    all_gather x1, blocking collectives, shards(): lax.all_gather(root_part.astype(jnp.bfloat16), 'col', axis=0, tiled=True)  23.4 us
  transfers between devices with their start and end apart: 8, of which 8 were waited for; matrix products, arithmetic and copies ran while one was open for 0% of the time, Pallas kernels for 0%

profile of v1, /device:TPU:32, one launch (start us, length us, event | category | flops | bytes accessed | tf_op | source)
XLA Modules:
  0.0 939.4 jit_solution(125207487583297875)
XLA Ops:
  9.1 2.7 fusion.15
  11.8 273.8 %while.37 = (s32[]{:T(128)}, f32[2048,128]{1,0:T(8,128)}, f32[128,128]{0,1:T(8,128)S(1)}, bf16[2,128,2048]{2,1,0:T(8,128)(2,1)}, s32[]{:T(128)}, /*index=5*/f32[...) while((s32[]{:T(128)}, f32[2048,128]{1,0:T(8,128)}, ...), condition=%wide.region_5.6_spmd.clone, body=%wide.region_0.5_spmd.clone.sunk | while | flops 474529792 | bytes 83624232 | solution.py:75
  11.9 1.1 broadcast_select_fusion.7
  13.0 121.4 %all-gather.6.cloned.1.call-done = f32[32768,128]{1,0:T(8,128)} async-done(((f32[2048,128]{1,0:T(8,128)}), f32[32768,128]{1,0:T(8,128)}) %all-gather.6.cloned.1.call-update) | async-done | bytes 16777232 | tf_op jit(solution)/shard_map/while/body/eval_jaxpr/all_gather | solution.py:59
  134.4 6.6 reduce_sum.15
  141.0 3.5 conditional.7
  141.1 3.5 convolution_bitcast_fusion.1
  144.6 3.4 psum.37
  148.0 2.4 convolution_add_fusion.4
  150.3 2.3 broadcast_select_fusion.7
  152.7 117.4 %all-gather.6.cloned.1.call-done = f32[32768,128]{1,0:T(8,128)} async-done(((f32[2048,128]{1,0:T(8,128)}), f32[32768,128]{1,0:T(8,128)}) %all-gather.6.cloned.1.call-update) | async-done | bytes 16777232 | tf_op jit(solution)/shard_map/while/body/eval_jaxpr/all_gather | solution.py:59
  270.0 6.6 reduce_sum.15
  276.7 6.5 psum.37
  283.3 2.4 convolution_add_fusion.4
  285.9 2.9 fusion.16
  289.8 253.0 %all-reduce.3.cloned.1.call-done = f32[1536,128]{1,0:T(8,128)} async-done(((f32[1536,128]{1,0:T(8,128)}), f32[1536,128]{1,0:T(8,128)}) %all-reduce.3.cloned.1.call-update) | async-done | bytes 786448 | tf_op jit(solution)/shard_map/psum | solution.py:89
  542.8 1.9 fusion.24
  545.5 1.2 copy.27
  546.8 79.1 %reduce-scatter.5.cloned.1.call-done = f32[96,128]{1,0:T(8,128)} async-done(((f32[1536,128]{1,0:T(8,128)}), f32[96,128]{1,0:T(8,128)}) %reduce-scatter.5.cloned.1.call-update) | async-done | bytes 49168 | tf_op jit(solution)/shard_map/reduce_scatter | solution.py:93
  626.7 23.4 %all_gather.27 = bf16[1536,128]{1,0:T(8,128)(2,1)S(1)} all-gather(bf16[96,128]{1,0:T(8,128)(2,1)S(1)} %convert_element_type.87), channel_id=1, replica_groups=mesh['sub'=8,'row'=2,'col'=16] {'col'}, dimensions={0}, use_global_device_ids=true | all-gather | bytes 417792 | tf_op jit(solution)/shard_map/all_gather | solution.py:105
  650.1 1.8 fusion.17
  652.3 278.9 %while.38 = (s32[]{:T(128)}, f32[128,128]{0,1:T(8,128)S(1)}, bf16[2048,128]{0,1:T(8,128)(2,1)S(1)}, s32[]{:T(128)}, bf16[2,128,2048]{2,1,0:T(8,128)(2,1)}, /*ind...) while((s32[]{:T(128)}, f32[128,128]{0,1:T(8,128)S(1)}, ...), condition=%wide.region_13.14_spmd.clone, body=%wide.region_8.13_spmd.clone.sunk | while | flops 470663168 | bytes 13697360 | solution.py:139
  652.4 2.0 convolution_add_fusion.5
  654.4 29.3 %all-reduce.5.cloned.1.call-done = f32[128,128]{1,0:T(8,128)} async-done(((f32[128,128]{1,0:T(8,128)}), f32[128,128]{1,0:T(8,128)}) %all-reduce.5.cloned.1.call-update) | async-done | bytes 65552 | tf_op jit(solution)/shard_map/while/body/eval_jaxpr/psum | solution.py:119
  684.9 81.8 %reduce-scatter.7.cloned.1.call-done = f32[128,128]{0,1:T(8,128)} async-done(((f32[2048,128]{0,1:T(8,128)}), f32[128,128]{0,1:T(8,128)}) %reduce-scatter.7.cloned.1.call-update) | async-done | bytes 65552 | tf_op jit(solution)/shard_map/while/body/eval_jaxpr/reduce_scatter | solution.py:132
  767.6 24.0 %all_gather.30 = bf16[2048,128]{0,1:T(8,128)(2,1)S(1)} all-gather(bf16[128,128]{0,1:T(8,128)(2,1)S(1)} %get-tuple-element.583), channel_id=1, replica_groups=mesh['sub'=8,'row'=2,'col'=16] {'col'}, dimensions={0}, use_global_device_ids=true | all-gather | bytes 557056 | tf_op jit(solution)/shard_map/while/body/eval_jaxpr/all_gather | solution.py:133
  792.0 2.0 convolution_add_fusion.5
  794.0 29.0 %all-reduce.5.cloned.1.call-done = f32[128,128]{1,0:T(8,128)} async-done(((f32[128,128]{1,0:T(8,128)}), f32[128,128]{1,0:T(8,128)}) %all-reduce.5.cloned.1.call-update) | async-done | bytes 65552 | tf_op jit(solution)/shard_map/while/body/eval_jaxpr/psum | solution.py:119
  823.0 1.9 conditional.8
  823.0 1.9 convolution_bitcast_fusion
  825.9 80.1 %reduce-scatter.7.cloned.1.call-done = f32[128,128]{0,1:T(8,128)} async-done(((f32[2048,128]{0,1:T(8,128)}), f32[128,128]{0,1:T(8,128)}) %reduce-scatter.7.cloned.1.call-update) | async-done | bytes 65552 | tf_op jit(solution)/shard_map/while/body/eval_jaxpr/reduce_scatter | solution.py:132
  906.9 24.0 %all_gather.30 = bf16[2048,128]{0,1:T(8,128)(2,1)S(1)} all-gather(bf16[128,128]{0,1:T(8,128)(2,1)S(1)} %get-tuple-element.583), channel_id=1, replica_groups=mesh['sub'=8,'row'=2,'col'=16] {'col'}, dimensions={0}, use_global_device_ids=true | all-gather | bytes 557056 | tf_op jit(solution)/shard_map/while/body/eval_jaxpr/all_gather | solution.py:133
  (64 shorter events, 9.9 us)
Async XLA Ops:
  8.0 534.8 %copy-start = (f32[96,1536]{1,0:T(8,128)S(1)}, f32[96,1536]{1,0:T(8,128)}, u32[]{:S(2)}) copy-start(f32[96,1536]{1,0:T(8,128)} %param.21) | copy-start | bytes 1769476
  11.8 273.8 %copy-start.4 = (bf16[1,1,128,1024]{3,2,1,0:T(8,128)(2,1)S(1)}, bf16[1,1,128,1024]{3,2,1,0:T(8,128)(2,1)}, u32[]{:S(2)}) copy-start(bf16[1,1,128,1024]{3,2,1,0:T(8,128)(2,1)} %param.19) | copy-start | bytes 786436
  11.8 274.0 %copy-start.7 = (s32[1,1024]{1,0:T(1,128)S(1)}, s32[1,1024]{1,0:T(1,128)}, u32[]{:S(2)}) copy-start(s32[1,1024]{1,0:T(1,128)} %param.20) | copy-start | bytes 12292
  11.8 122.5 %all-gather.6.cloned.1.call-start = ((), (), s32[]{:S(2)}) async-start(), calls=%async_computation.4 | async-start | bytes 17825792 | tf_op jit(solution)/shard_map/while/body/eval_jaxpr/all_gather | solution.py:59
  141.0 6.9 copy-start.1
  150.3 119.7 %all-gather.6.cloned.1.call-start = ((), (), s32[]{:S(2)}) async-start(), calls=%async_computation.4 | async-start | bytes 17825792 | tf_op jit(solution)/shard_map/while/body/eval_jaxpr/all_gather | solution.py:59
  276.7 6.6 copy-start.1
  285.6 257.2 %all-reduce.3.cloned.1.call-start = ((), (), s32[]{:S(2)}) async-start(), calls=%async_computation.2 | async-start | bytes 1572864 | tf_op jit(solution)/shard_map/psum | solution.py:89
  285.9 2.9 copy-start.6
  288.8 0.9 copy-start.5
  289.8 336.2 %reduce-scatter.5.cloned.1.call-start = ((), (), s32[]{:S(2)}) async-start(), calls=%async_computation.3 | async-start | bytes 835584 | tf_op jit(solution)/shard_map/reduce_scatter | solution.py:93
  650.1 2.2 copy-start.2
  652.3 31.4 %all-reduce.5.cloned.1.call-start = ((), (), s32[]{:S(2)}) async-start(), calls=%async_computation.5 | async-start | bytes 131072 | tf_op jit(solution)/shard_map/while/body/eval_jaxpr/psum | solution.py:119
  654.4 112.3 %reduce-scatter.7.cloned.1.call-start = ((), (), s32[]{:S(2)}) async-start(), calls=%async_computation.6 | async-start | bytes 1114112 | tf_op jit(solution)/shard_map/while/body/eval_jaxpr/reduce_scatter | solution.py:132
  683.9 1.0 copy-start.3
  791.9 31.1 %all-reduce.5.cloned.1.call-start = ((), (), s32[]{:S(2)}) async-start(), calls=%async_computation.5 | async-start | bytes 131072 | tf_op jit(solution)/shard_map/while/body/eval_jaxpr/psum | solution.py:119
  794.0 112.0 %reduce-scatter.7.cloned.1.call-start = ((), (), s32[]{:S(2)}) async-start(), calls=%async_computation.6 | async-start | bytes 1114112 | tf_op jit(solution)/shard_map/while/body/eval_jaxpr/reduce_scatter | solution.py:132
  824.9 1.0 copy-start.3
Sparse Core Ops, SparseCore 0:
  15.4 118.9 all-gather.5
  153.9 116.0 all-gather.5
  656.4 27.2 all-reduce.4
  687.5 79.1 reduce-scatter.6
  795.7 27.2 all-reduce.4
  826.8 79.1 reduce-scatter.6
Sparse Core Ops, SparseCore 1:
  291.5 251.2 all-reduce.2
  547.1 78.7 reduce-scatter.4
